TPU v7x, 512 devices: a whole 4x4x16 slice. The times are simulated.
512 devices in a mesh: seq: 64 (over y, z), head: 8 (over x, core).
Axes of the slice: x: 4, y: 4, z: 16, core: 2. Of those that a mesh axis runs over, the one named last changes fastest.
Arguments:
- hidden_in: bfloat16 [16384, 4096], P('seq', 'head'), may hold values from -6 to 6
- proj_weight: bfloat16 [4096, 256], replicated, may hold values from -0.09375 to 0.09375
- head_input: bfloat16 [16384, 8192], P('seq', 'head'), may hold values from -6 to 6
- gate_input: bfloat16 [16384, 8192], P('seq', 'head'), may hold values from -11 to 11
- step_size: float32 [16384, 128], P('seq', 'head'), may hold values from 0 to 4, as said below
- decay_rate: float32 [128], P('head'), may hold values from 0 to 1, as said below
- norm_gain: float32 [8192], P('head'), may hold values from 0.1 to 1.9
Outputs:
- layer_out: bfloat16 [16384, 8192], P('seq', 'head')
Inputs may be any that keep to these rules, and one draw needn't show every extreme that they name: `decay_rate`: positive. `step_size`: positive.
All inputs are finite; a program needn't handle non-finite values.
Results may differ from a plain program's by a relative error of at most 0.013.
Values may be sent and summed in bfloat16 or wider, within the bound.
A program may use at most 128 MiB of HBM per device.

v0:
```python
import jax
import jax.numpy as jnp
from jax import lax
from jax.sharding import PartitionSpec as P

HEADS = 128
HEAD_DIM = 64
STATE = 128
GROUP = 256


def carried_in(value, axis, join, neutral):
    count, mine = (lax.axis_size(axis), lax.axis_index(axis))
    pieces = jax.tree.map(lambda part: lax.all_gather(part, axis), value)
    running = jax.tree.map(
        lambda part, zero: jnp.full_like(part, 0) + jnp.asarray(zero, part.dtype), value, neutral
    )

    def step(position, running):
        longer = join(running, jax.tree.map(lambda part: part[position], pieces))
        return jax.tree.map(lambda new, old: jnp.where(position < mine, new, old), longer, running)

    return lax.fori_loop(0, count - 1, step, running)


def combine_states(earlier, later):
    return (earlier[0] + later[0], jnp.exp(later[0])[:, None, None] * earlier[1] + later[1])


def shards(hidden_in, proj_weight, head_input, gate_input, step_size, decay_rate, norm_gain):
    tok_rows = hidden_in.shape[0]
    local_heads = step_size.shape[1]
    summed = jnp.dot(
        lax.all_gather(hidden_in, "head", axis=1, tiled=True),
        proj_weight,
        preferred_element_type=jnp.float32,
    )
    projected = summed.astype(jnp.bfloat16)
    count = tok_rows // GROUP
    b_rows = projected[:, :STATE].reshape(count, GROUP, STATE)
    c_rows = projected[:, STATE:].reshape(count, GROUP, STATE)
    log_decay = -step_size * decay_rate[None, :]
    cumulative = jnp.cumsum(log_decay.reshape(count, GROUP, local_heads), axis=1)
    scaled = (
        head_input.reshape(tok_rows, local_heads, HEAD_DIM).astype(jnp.float32)
        * step_size[:, :, None]
    ).astype(jnp.bfloat16)
    scaled = scaled.reshape(count, GROUP, local_heads, HEAD_DIM)
    positions = jnp.arange(GROUP, dtype=jnp.int32)
    causal = positions[:, None] >= positions[None, :]
    scores = jnp.einsum("ctn,csn->cts", c_rows, b_rows, preferred_element_type=jnp.float32)
    cum_heads = jnp.swapaxes(cumulative, 1, 2)
    gap = cum_heads[:, :, :, None] - cum_heads[:, :, None, :]
    weights = jnp.exp(jnp.where(causal[None, None], gap, -jnp.inf))
    mixing = (scores[:, None] * weights).astype(jnp.bfloat16)
    inner = jnp.einsum("chts,cshp->cthp", mixing, scaled, preferred_element_type=jnp.float32)
    ends = cumulative[:, -1, :]
    tail = jnp.exp(ends[:, None, :] - cumulative)
    weighted = (tail[:, :, :, None] * scaled.astype(jnp.float32)).astype(jnp.bfloat16)
    fresh = jnp.einsum("cshp,csn->chpn", weighted, b_rows, preferred_element_type=jnp.float32)
    block_state = jnp.zeros((local_heads, HEAD_DIM, STATE), jnp.float32)
    block_state = jnp.exp(ends[0])[:, None, None] * block_state + fresh[0]
    block_decay = jnp.sum(ends, axis=0)
    identity = (
        jnp.zeros((local_heads,), jnp.float32),
        jnp.zeros((local_heads, HEAD_DIM, STATE), jnp.float32),
    )
    decay_total, incoming = carried_in((block_decay, block_state), "seq", combine_states, identity)
    entering = [incoming]
    carried_low = jnp.stack(entering).astype(jnp.bfloat16)
    outer = jnp.einsum("ctn,chpn->cthp", c_rows, carried_low, preferred_element_type=jnp.float32)
    outer = outer * jnp.exp(cumulative)[:, :, :, None]
    mixed = (inner + outer).reshape(tok_rows, local_heads * HEAD_DIM)
    gated = mixed * jax.nn.silu(gate_input.astype(jnp.float32))
    squares = jnp.sum(gated * gated, axis=1)
    total_squares = lax.psum(squares, "head")
    mean_square = total_squares / (HEADS * HEAD_DIM)
    return (gated * lax.rsqrt(mean_square + 1e-05)[:, None] * norm_gain[None, :]).astype(
        jnp.bfloat16
    )


def solution(mesh):
    in_specs = (
        P("seq", "head"),
        P(),
        P("seq", "head"),
        P("seq", "head"),
        P("seq", "head"),
        P("head"),
        P("head"),
    )
    out_specs = P("seq", "head")
    return jax.shard_map(shards, mesh=mesh, in_specs=in_specs, out_specs=out_specs, check_vma=False)
```

profile of v0, /device:TPU:1, one launch (start us, length us, event | category | flops | bytes accessed | tf_op | source)
XLA Modules:
  0.0 524.2 jit_solution(10919568476322371059)
XLA Ops:
  9.5 1.2 copy.29
  11.6 36.5 %all-gather.5.cloned.1.call-done = bf16[256,4096]{1,0:T(8,128)(2,1)} async-done(((bf16[256,512]{1,0:T(8,128)(2,1)}), bf16[256,4096]{1,0:T(8,128)(2,1)}) %all-gather.5.cloned.1.call-update) | async-done | bytes 2097168 | tf_op jit(solution)/shard_map/all_gather | solution.py:34
  48.1 2.3 convolution_convert_fusion
  52.3 70.7 %all-gather = f32[64,1,16]{2,1,0:T(1,128)} all-gather(f32[1,1,16]{2,1,0:T(1,128)S(1)} %copy.34), channel_id=2, replica_groups=mesh['seq'=64,'head'=8] {'seq'}, dimensions={0}, use_global_device_ids=true | all-gather | bytes 4160 | tf_op jit(solution)/shard_map/all_gather | solution.py:14
  124.5 219.6 %all-gather.7.cloned.1.call-done = f32[1024,64,128]{2,1,0:T(8,128)} async-done(((f32[16,64,128]{2,1,0:T(8,128)}), f32[1024,64,128]{2,1,0:T(8,128)}) %all-gather.7.cloned.1.call-update) | async-done | bytes 33554448 | tf_op jit(solution)/shard_map/all_gather | solution.py:14
  344.1 150.7 %while.14 = (s32[]{:T(128)}, f32[16,64,128]{2,1,0:T(8,128)S(1)}, s32[]{:T(128)}, f32[64,16]{1,0:T(8,128)}, f32[64,16,64,128]{3,2,1,0:T(8,128)}, /*index=5*/s32[]{:T(128)}, s32[]{:T(128)}) while((s32[]{:T(128)}, f32[16,64,128]{2,1,0:T(8,128)S(1)}, s32[]{:T(128)}, f32[64,16]{1,0:T(8,128)}, f32[64,16,64,128]{3,2,1,0:T(8,128)}, ...), condition=%wide.region_3.4_spmd.clone, body=%wide.region_2.3_spmd.clone.sunk | while | flops 524292 | bytes 1573161 | solution.py:23
  344.1 1.2 exponential_bitcast_fusion.2
  346.5 1.2 exponential_bitcast_fusion.2
  348.9 1.2 exponential_bitcast_fusion.2
  351.3 1.2 exponential_bitcast_fusion.2
  353.7 1.2 exponential_bitcast_fusion.2
  356.1 1.2 exponential_bitcast_fusion.2
  358.5 1.2 exponential_bitcast_fusion.2
  360.9 1.2 exponential_bitcast_fusion.2
  363.2 1.2 exponential_bitcast_fusion.2
  365.6 1.2 exponential_bitcast_fusion.2
  368.0 1.2 exponential_bitcast_fusion.2
  370.4 1.2 exponential_bitcast_fusion.2
  372.8 1.2 exponential_bitcast_fusion.2
  375.2 1.2 exponential_bitcast_fusion.2
  377.6 1.2 exponential_bitcast_fusion.2
  380.0 1.2 exponential_bitcast_fusion.2
  382.4 1.2 exponential_bitcast_fusion.2
  384.8 1.2 exponential_bitcast_fusion.2
  387.2 1.2 exponential_bitcast_fusion.2
  389.6 1.2 exponential_bitcast_fusion.2
  392.0 1.2 exponential_bitcast_fusion.2
  394.4 1.2 exponential_bitcast_fusion.2
  401.5 1.2 exponential_bitcast_fusion.2
  403.9 1.2 exponential_bitcast_fusion.2
  406.3 1.2 exponential_bitcast_fusion.2
  408.7 1.2 exponential_bitcast_fusion.2
  411.1 1.2 exponential_bitcast_fusion.2
  413.5 1.2 exponential_bitcast_fusion.2
  415.9 1.2 exponential_bitcast_fusion.2
  418.3 1.2 exponential_bitcast_fusion.2
  420.6 1.2 exponential_bitcast_fusion.2
  423.0 1.2 exponential_bitcast_fusion.2
  425.4 1.2 exponential_bitcast_fusion.2
  427.8 1.2 exponential_bitcast_fusion.2
  430.2 1.2 exponential_bitcast_fusion.2
  432.6 1.2 exponential_bitcast_fusion.2
  435.0 1.2 exponential_bitcast_fusion.2
  437.4 1.2 exponential_bitcast_fusion.2
  458.8 1.2 exponential_bitcast_fusion.2
  461.2 1.2 exponential_bitcast_fusion.2
  463.6 1.2 exponential_bitcast_fusion.2
  466.0 1.2 exponential_bitcast_fusion.2
  468.4 1.2 exponential_bitcast_fusion.2
  470.8 1.2 exponential_bitcast_fusion.2
  473.2 1.2 exponential_bitcast_fusion.2
  475.6 1.2 exponential_bitcast_fusion.2
  478.0 1.2 exponential_bitcast_fusion.2
  480.4 1.2 exponential_bitcast_fusion.2
  482.8 1.2 exponential_bitcast_fusion.2
  485.2 1.2 exponential_bitcast_fusion.2
  487.6 1.2 exponential_bitcast_fusion.2
  490.0 1.2 exponential_bitcast_fusion.2
  492.4 1.2 exponential_bitcast_fusion.2
  495.8 3.1 fusion.9
  498.9 1.6 copy.37
  500.5 1.4 multiply_reduce_fusion
  501.9 13.2 %psum.7 = f32[256]{0:T(256)S(1)} all-reduce(f32[256]{0:T(256)S(1)} %multiply_reduce_fusion), channel_id=1, replica_groups=mesh['seq'=64,'head'=8] {'head'}, use_global_device_ids=true, to_apply=%region_5.6 | all-reduce | flops 256 | bytes 2048 | tf_op jit(solution)/shard_map/psum | solution.py:76
  515.1 2.2 multiply_convert_fusion.6
  (107 shorter events, 93.7 us)
Async XLA Ops:
  6.5 41.6 %copy-start = (bf16[4096,256]{1,0:T(8,128)(2,1)S(1)}, bf16[4096,256]{1,0:T(8,128)(2,1)}, u32[]{:S(2)}) copy-start(bf16[4096,256]{1,0:T(8,128)(2,1)} %param.10) | copy-start | bytes 6291460
  6.5 41.6 %all-gather.5.cloned.1.call-start = ((), (), s32[]{:S(2)}) async-start(), calls=%async_computation | async-start | bytes 2359296 | tf_op jit(solution)/shard_map/all_gather | solution.py:34
  7.3 336.8 %all-gather.7.cloned.1.call-start = ((), (), s32[]{:S(2)}) async-start(), calls=%async_computation.1 | async-start | bytes 34078720 | tf_op jit(solution)/shard_map/all_gather | solution.py:14
  344.1 151.7 %copy-start.1 = (f32[256,16]{0,1:T(8,128)S(1)}, f32[256,16]{0,1:T(8,128)}, u32[]{:S(2)}) copy-start(f32[256,16]{0,1:T(8,128)} %param.13) | copy-start | bytes 49156
  495.8 19.3 %copy-start.2 = (f32[1024]{0:T(1024)S(1)}, f32[1024]{0:T(1024)}, u32[]{:S(2)}) copy-start(f32[1024]{0:T(1024)} %param.15) | copy-start | bytes 12292
Sparse Core Ops, SparseCore 0:
  9.5 38.6 all-gather.4
  51.7 292.3 all-gather.6
where the time goes:
time: 528 us; the launch traced here: 524 us
  waiting for transfers between devices  257 us (49%)
  blocking collectives  83.9 us (16%)
  other arithmetic  81 us (15%)
  local copies, waits for them, and re-layouts  79.9 us (15%)
  between operations  13.5 us (3%)
  matrix products  7.67 us (1%)
    all_gather x1, waiting for transfers between devices, carried_in(): pieces = jax.tree.map(lambda part: lax.all_gather(part, axis), value)  220 us
    exp x63, local copies, waits for them, and re-layouts, combine_states(): jnp.exp(later[0])[:, None, None] * earlier[1] + later[1]  75.8 us
    select_n x63, other arithmetic, step(): jnp.where(position < mine, new, old)  73.7 us
    all_gather x1, blocking collectives, carried_in(): pieces = jax.tree.map(lambda part: lax.all_gather(part, axis), value)  70.7 us
    all_gather x1, waiting for transfers between devices, shards(): lax.all_gather(hidden_in, 'head', axis=1, tiled=True)  36.5 us
    psum x1, blocking collectives, shards(): total_squares = lax.psum(squares, 'head')  13.2 us
  transfers between devices with their start and end apart: 2, of which 2 were waited for; matrix products, arithmetic and copies ran while one was open for 1% of the time, Pallas kernels for 0%

commit v1 on v0

--- a/solution.py
+++ b/solution.py
@@ -31,7 +31,9 @@
     tok_rows = hidden_in.shape[0]
     local_heads = step_size.shape[1]
     summed = jnp.dot(
-        lax.all_gather(hidden_in, "head", axis=1, tiled=True),
+        jnp.concatenate(
+            lax.all_to_all(jnp.stack([hidden_in] * lax.axis_size("head")), "head", 0, 0), axis=1
+        ),
         proj_weight,
         preferred_element_type=jnp.float32,
     )

time: 528 us -> 524 us (level)
  waiting for transfers between devices: 257 us -> 243 us
  starting transfers between devices: 0.04 us -> 11.2 us
    all_gather x1 -> x0, waiting for transfers between devices: 36.5 us -> none  [shards(): lax.all_gather(hidden_in, 'head', axis=1, tiled=True)]
    all_to_all x0 -> x1, waiting for transfers between devices: none -> 24.5 us  [shards(): lax.all_to_all(jnp.stack([hidden_in] * lax.axis_size('head')), 'head', 0, 0)]
    all_to_all x0 -> x1, starting transfers between devices: none -> 11.2 us  [shards(): lax.all_to_all(jnp.stack([hidden_in] * lax.axis_size('head')), 'head', 0, 0)]
where the time goes in v1:
time: 524 us; the launch traced here: 520 us
  waiting for transfers between devices  243 us (46%)
  blocking collectives  82.2 us (16%)
  local copies, waits for them, and re-layouts  81.5 us (16%)
  other arithmetic  79.6 us (15%)
  between operations  13.5 us (3%)
  starting transfers between devices  11.2 us (2%)
  matrix products  7.73 us (1%)
    all_gather x1, waiting for transfers between devices, carried_in(): pieces = jax.tree.map(lambda part: lax.all_gather(part, axis), value)  219 us
    exp x63, local copies, waits for them, and re-layouts, combine_states(): jnp.exp(later[0])[:, None, None] * earlier[1] + later[1]  75.8 us
    select_n x63, other arithmetic, step(): jnp.where(position < mine, new, old)  73.7 us
    all_gather x1, blocking collectives, carried_in(): pieces = jax.tree.map(lambda part: lax.all_gather(part, axis), value)  69 us
    all_to_all x1, waiting for transfers between devices, shards(): lax.all_to_all(jnp.stack([hidden_in] * lax.axis_size('head')), 'head', 0, 0)  24.5 us
    psum x1, blocking collectives, shards(): total_squares = lax.psum(squares, 'head')  13.2 us
    all_to_all x1, starting transfers between devices, shards(): lax.all_to_all(jnp.stack([hidden_in] * lax.axis_size('head')), 'head', 0, 0)  11.2 us
  transfers between devices with their start and end apart: 2, of which 2 were waited for; matrix products, arithmetic and copies ran while one was open for 1% of the time, Pallas kernels for 0%

profile of v1, /device:TPU:1, one launch (start us, length us, event | category | flops | bytes accessed | tf_op | source)
XLA Modules:
  0.0 520.3 jit_solution(12702129873526778517)
XLA Ops:
  6.5 1.2 copy.32
  7.8 1.4 stack.2
  9.2 11.2 %all-to-all-start = ((bf16[8,256,512]{1,2,0:T(8,128)(2,1)}), bf16[8,256,512]{1,2,0:T(8,128)(2,1)}, u32[]{:S(2)}, u32[]{:S(2)}) async-start(bf16[8,256,512]{1,2,0:T(8,128)(2,1)} %stack.2), calls=%async_computation | async-start | bytes 4194304 | tf_op jit(solution)/shard_map/all_to_all | solution.py:35
  22.3 24.5 %all-to-all-done = bf16[8,256,512]{1,2,0:T(8,128)(2,1)} async-done(((bf16[8,256,512]{1,2,0:T(8,128)(2,1)}), bf16[8,256,512]{1,2,0:T(8,128)(2,1)}, u32[]{:S(2)}, u32[]{:S(2)}) %all-to-all-start) | async-done | bytes 2097184 | tf_op jit(solution)/shard_map/all_to_all | solution.py:35
  46.7 2.3 convolution_convert_fusion
  50.9 69.0 %all-gather = f32[64,1,16]{2,1,0:T(1,128)} all-gather(f32[1,1,16]{2,1,0:T(1,128)S(1)} %copy.37), channel_id=2, replica_groups=mesh['seq'=64,'head'=8] {'seq'}, dimensions={0}, use_global_device_ids=true | all-gather | bytes 4160 | tf_op jit(solution)/shard_map/all_gather | solution.py:14
  121.4 218.8 %all-gather.4.cloned.1.call-done = f32[1024,64,128]{2,1,0:T(8,128)} async-done(((f32[16,64,128]{2,1,0:T(8,128)}), f32[1024,64,128]{2,1,0:T(8,128)}) %all-gather.4.cloned.1.call-update) | async-done | bytes 33554448 | tf_op jit(solution)/shard_map/all_gather | solution.py:14
  340.2 150.7 %while.14 = (s32[]{:T(128)}, f32[16,64,128]{2,1,0:T(8,128)S(1)}, s32[]{:T(128)}, f32[64,16]{1,0:T(8,128)}, f32[64,16,64,128]{3,2,1,0:T(8,128)}, /*index=5*/s32[]{:T(128)}, s32[]{:T(128)}) while((s32[]{:T(128)}, f32[16,64,128]{2,1,0:T(8,128)S(1)}, s32[]{:T(128)}, f32[64,16]{1,0:T(8,128)}, f32[64,16,64,128]{3,2,1,0:T(8,128)}, ...), condition=%wide.region_3.4_spmd.clone, body=%wide.region_2.3_spmd.clone.sunk | while | flops 524292 | bytes 1573161 | solution.py:23
  340.2 1.2 exponential_bitcast_fusion.2
  342.6 1.2 exponential_bitcast_fusion.2
  345.0 1.2 exponential_bitcast_fusion.2
  347.4 1.2 exponential_bitcast_fusion.2
  349.8 1.2 exponential_bitcast_fusion.2
  352.2 1.2 exponential_bitcast_fusion.2
  354.6 1.2 exponential_bitcast_fusion.2
  357.0 1.2 exponential_bitcast_fusion.2
  359.4 1.2 exponential_bitcast_fusion.2
  361.8 1.2 exponential_bitcast_fusion.2
  364.2 1.2 exponential_bitcast_fusion.2
  366.6 1.2 exponential_bitcast_fusion.2
  369.0 1.2 exponential_bitcast_fusion.2
  371.4 1.2 exponential_bitcast_fusion.2
  373.8 1.2 exponential_bitcast_fusion.2
  376.2 1.2 exponential_bitcast_fusion.2
  378.6 1.2 exponential_bitcast_fusion.2
  380.9 1.2 exponential_bitcast_fusion.2
  383.3 1.2 exponential_bitcast_fusion.2
  385.7 1.2 exponential_bitcast_fusion.2
  397.7 1.2 exponential_bitcast_fusion.2
  400.0 1.2 exponential_bitcast_fusion.2
  402.4 1.2 exponential_bitcast_fusion.2
  404.8 1.2 exponential_bitcast_fusion.2
  407.2 1.2 exponential_bitcast_fusion.2
  409.6 1.2 exponential_bitcast_fusion.2
  412.0 1.2 exponential_bitcast_fusion.2
  414.4 1.2 exponential_bitcast_fusion.2
  416.8 1.2 exponential_bitcast_fusion.2
  419.2 1.2 exponential_bitcast_fusion.2
  421.6 1.2 exponential_bitcast_fusion.2
  423.9 1.2 exponential_bitcast_fusion.2
  426.3 1.2 exponential_bitcast_fusion.2
  428.7 1.2 exponential_bitcast_fusion.2
  431.1 1.2 exponential_bitcast_fusion.2
  433.5 1.2 exponential_bitcast_fusion.2
  455.0 1.2 exponential_bitcast_fusion.2
  457.4 1.2 exponential_bitcast_fusion.2
  459.8 1.2 exponential_bitcast_fusion.2
  462.2 1.2 exponential_bitcast_fusion.2
  464.6 1.2 exponential_bitcast_fusion.2
  466.9 1.2 exponential_bitcast_fusion.2
  469.3 1.2 exponential_bitcast_fusion.2
  471.7 1.2 exponential_bitcast_fusion.2
  474.1 1.2 exponential_bitcast_fusion.2
  476.5 1.2 exponential_bitcast_fusion.2
  478.9 1.2 exponential_bitcast_fusion.2
  481.3 1.2 exponential_bitcast_fusion.2
  483.7 1.2 exponential_bitcast_fusion.2
  486.1 1.2 exponential_bitcast_fusion.2
  488.5 1.2 exponential_bitcast_fusion.2
  491.9 3.1 fusion.9
  495.0 1.6 copy.40
  496.6 1.4 multiply_reduce_fusion
  498.1 13.2 %psum.7 = f32[256]{0:T(256)S(1)} all-reduce(f32[256]{0:T(256)S(1)} %multiply_reduce_fusion), channel_id=1, replica_groups=mesh['seq'=64,'head'=8] {'head'}, use_global_device_ids=true, to_apply=%region_5.6 | all-reduce | flops 256 | bytes 2048 | tf_op jit(solution)/shard_map/psum | solution.py:78
  511.2 2.2 multiply_convert_fusion.6
  (112 shorter events, 94.2 us)
Async XLA Ops:
  6.5 40.2 %copy-start = (bf16[4096,256]{1,0:T(8,128)(2,1)S(1)}, bf16[4096,256]{1,0:T(8,128)(2,1)}, u32[]{:S(2)}) copy-start(bf16[4096,256]{1,0:T(8,128)(2,1)} %param.10) | copy-start | bytes 6291460
  9.2 11.2 %copy-start.2 = (f32[256,16]{0,1:T(8,128)S(1)}, f32[256,16]{0,1:T(8,128)}, u32[]{:S(2)}) copy-start(f32[256,16]{0,1:T(8,128)} %param.13) | copy-start | bytes 49156
  9.2 11.2 %copy-start.4 = (f32[16]{0:T(128)S(1)}, f32[16]{0:T(128)}, u32[]{:S(2)}) copy-start(f32[16]{0:T(128)} %param.14) | copy-start | bytes 196
  9.2 12.7 %copy-start.1 = (bf16[256,1024]{1,0:T(8,128)(2,1)S(1)}, bf16[256,1024]{1,0:T(8,128)(2,1)}, u32[]{:S(2)}) copy-start(bf16[256,1024]{1,0:T(8,128)(2,1)} %param.11) | copy-start | bytes 1572868
  9.2 37.5 %all-to-all-start = ((bf16[8,256,512]{1,2,0:T(8,128)(2,1)}), bf16[8,256,512]{1,2,0:T(8,128)(2,1)}, u32[]{:S(2)}, u32[]{:S(2)}) async-start(bf16[8,256,512]{1,2,0:T(8,128)(2,1)} %stack.2), calls=%async_computation | async-start | bytes 4194304 | tf_op jit(solution)/shard_map/all_to_all | solution.py:35
  20.4 319.8 %all-gather.4.cloned.1.call-start = ((), (), s32[]{:S(2)}) async-start(), calls=%async_computation.1 | async-start | bytes 34078720 | tf_op jit(solution)/shard_map/all_gather | solution.py:14
  495.0 16.2 %copy-start.3 = (f32[1024]{0:T(1024)S(1)}, f32[1024]{0:T(1024)}, u32[]{:S(2)}) copy-start(f32[1024]{0:T(1024)} %param.15) | copy-start | bytes 12292
Sparse Core Ops, SparseCore 0:
  50.3 289.8 all-gather.3
